TPU v7x, 32 devices: a whole 2x2x4 slice. The times are simulated.
32 devices in a mesh: expert: 32 (over z, y, x, core).
Axes of the slice: x: 2, y: 2, z: 4, core: 2. Of those that a mesh axis runs over, the one named last changes fastest.
Arguments:
- tokens: bfloat16 [4096, 3584], P('expert'), may hold values from -6 to 6
- cotangent: bfloat16 [4096, 3584], P('expert'), may hold values from -6 to 6
- routes: int32 [4096, 8], P('expert'), may hold values from 0 to 15, all different within a row; in each aligned block of 128 rows (0 to 127, 128 to 255, ...) at most 80 rows name the same one
- gates: bfloat16 [4096, 8], P('expert'), may hold values from 0.049804688 to 0.29882812
- previous_row: int32 [16], replicated, may hold values from 0 to 15, each once
- gu_payload: bfloat16 [16, 3584, 2048], P(None, 'expert'), may hold values from -0.09375 to 0.09375
- gu_scales: float32 [16, 28, 16], replicated, may hold values from 0.5 to 2
- down_payload: bfloat16 [16, 1024, 3584], P(None, 'expert'), may hold values from -0.1875 to 0.1875
- down_scales: float32 [16, 8, 28], replicated, may hold values from 0.5 to 2
Outputs:
- layer_out: bfloat16 [4096, 3584], P('expert')
- gate_grad: float32 [4096, 8], P('expert')
Inputs may be any that keep to these rules, and one draw needn't show every extreme that they name: `routes`: each token names 8 different experts; among the tokens of one device no expert is named by more than 80 of them, and in some devices' tokens one expert is named by exactly 80. `previous_row`: each stored row holds exactly one expert.
All inputs are finite; a program needn't handle non-finite values.
Results may differ from a plain program's by a relative error of at most 0.0076.
Values may be sent and summed in bfloat16 or wider, within the bound.
A program may use at most 256 MiB of HBM per device.

v0:
```python
import jax
import jax.numpy as jnp
from jax import lax
from jax.sharding import PartitionSpec as P


def dequantize(payload, scales):
    expanded = jnp.repeat(jnp.repeat(scales, 128, axis=0), 128, axis=1)
    return (payload.astype(jnp.float32) * expanded).astype(jnp.bfloat16)


def plan(routes, gates, previous_row, most):
    local_count = routes.shape[0]
    rows = previous_row.shape[0]
    ids = jnp.arange(rows, dtype=jnp.int32)
    row_of = jnp.sum(jnp.where(routes[:, :, None] == ids, previous_row, 0), axis=2)
    hits = row_of[:, :, None] == ids
    chosen = jnp.sum(hits.astype(jnp.float32), axis=1)
    gate_of = jnp.sum(jnp.where(hits, gates.astype(jnp.float32)[:, :, None], 0.0), axis=1)
    places = jnp.arange(local_count, dtype=jnp.int32)
    before = (places[:, None] < places[None, :]).astype(jnp.bfloat16)
    rank = jnp.einsum(
        "ut,us->st", before, chosen.astype(jnp.bfloat16), preferred_element_type=jnp.float32
    ).astype(jnp.int32)
    slots = jnp.arange(most, dtype=jnp.int32)
    picked = (rank[:, None, :] == slots[None, :, None]) & (chosen.T[:, None, :] > 0)
    select = picked.astype(jnp.bfloat16)
    weigh = jnp.where(picked, gate_of.T[:, None, :], 0.0).astype(jnp.bfloat16)
    return hits, select.reshape(rows * most, local_count), weigh.reshape(rows * most, local_count)


def shards(
    tokens, cotangent, routes, gates, previous_row, gu_payload, gu_scales, down_payload, down_scales
):
    local_count, model_width = tokens.shape
    top = routes.shape[1]
    hidden_width = gu_payload.shape[2] // 2
    devices = lax.axis_size("expert")
    device_id = lax.axis_index("expert")
    experts = previous_row.shape[0]
    copies = devices // experts
    groups = [[c * experts + i for i in range(experts)] for c in range(copies)]
    most = local_count * top * 5 // (4 * experts)
    hits, select, weigh = plan(routes, gates, previous_row, most)
    outgoing = jnp.dot(select, tokens, preferred_element_type=jnp.float32).astype(jnp.bfloat16)
    outgoing = outgoing.reshape(experts, most, model_width)
    arrived = lax.all_to_all(
        outgoing, "expert", split_axis=0, concat_axis=0, tiled=True, axis_index_groups=groups
    )
    send_gate = jnp.concatenate([gu_payload] * copies, axis=0)
    send_down = jnp.concatenate([down_payload] * copies, axis=0)
    got_gate = lax.all_to_all(send_gate, "expert", split_axis=0, concat_axis=0, tiled=True)
    got_down = lax.all_to_all(send_down, "expert", split_axis=0, concat_axis=0, tiled=True)
    own_row = device_id % experts
    w_gu = dequantize(got_gate.reshape(model_width, 2 * hidden_width), gu_scales[own_row])
    w_down = dequantize(got_down.reshape(hidden_width, model_width), down_scales[own_row])
    row_block = arrived.reshape(-1, model_width)
    hidden = jnp.dot(row_block, w_gu, preferred_element_type=jnp.float32)
    active = (jax.nn.silu(hidden[:, :hidden_width]) * hidden[:, hidden_width:]).astype(jnp.bfloat16)
    result = jnp.dot(active, w_down, preferred_element_type=jnp.float32).astype(jnp.bfloat16)
    returned = lax.all_to_all(
        result.reshape(arrived.shape),
        "expert",
        split_axis=0,
        concat_axis=0,
        tiled=True,
        axis_index_groups=groups,
    ).reshape(-1, model_width)
    layer_out = jnp.einsum(
        "st,sd->td", weigh, returned, preferred_element_type=jnp.float32
    ).astype(jnp.bfloat16)
    dots = jnp.einsum("sd,td->st", returned, cotangent, preferred_element_type=jnp.float32)
    dots = jnp.sum(
        jnp.where(select > 0, dots, 0.0).reshape(experts, most, local_count), axis=1
    )
    gate_grad = jnp.sum(jnp.where(hits, dots.T[:, None, :], 0.0), axis=2)
    return (layer_out, gate_grad)


def solution(mesh):
    in_specs = (
        P("expert", None),
        P("expert", None),
        P("expert", None),
        P("expert", None),
        P(),
        P(None, "expert", None),
        P(),
        P(None, "expert", None),
        P(),
    )
    out_specs = (P("expert", None), P("expert", None))
    return jax.shard_map(shards, mesh=mesh, in_specs=in_specs, out_specs=out_specs, check_vma=False)
```

profile of v0, /device:TPU:16, one launch (start us, length us, event | category | flops | bytes accessed | tf_op | source)
XLA Modules:
  0.0 829.8 jit_solution(14591731127316050223)
XLA Ops:
  0.6 0.9 select_reduce_fusion.2
  1.8 0.2 fusion.11
  2.0 6.0 convolution_convert_fusion.1
  8.1 4.9 all-to-all-start
  13.0 13.1 %pad_maximum_fusion = bf16[32,112,2048]{2,1,0:T(8,128)(2,1)} fusion(bf16[16,112,2048]{2,1,0:T(8,128)(2,1)} %param.14), kind=kLoop, calls=%fused_computation.7 | loop fusion | flops 7340032 | bytes 22020096 | tf_op jit(solution)/shard_map/concatenate | solution.py:50
  26.1 127.8 %all-to-all-done = bf16[16,80,3584]{2,1,0:T(8,128)(2,1)} async-done(((bf16[16,80,3584]{2,1,0:T(8,128)(2,1)}), bf16[16,80,3584]{2,1,0:T(8,128)(2,1)}, u32[]{:S(2)}, u32[]{:S(2)}) %all-to-all-start) | async-done | bytes 9175072 | tf_op jit(solution)/shard_map/all_to_all | solution.py:47
  153.8 6.7 all-to-all-start.1
  160.6 6.7 pad_maximum_fusion.1
  167.3 316.1 %all-to-all-done.1 = bf16[32,112,2048]{2,1,0:T(8,128)(2,1)} async-done(((bf16[32,112,2048]{2,1,0:T(8,128)(2,1)}), bf16[32,112,2048]{2,1,0:T(8,128)(2,1)}, u32[]{:S(2)}, u32[]{:S(2)}) %all-to-all-start.1) | async-done | bytes 14680096 | tf_op jit(solution)/shard_map/all_to_all | solution.py:52
  483.3 6.7 all-to-all-start.2
  490.1 0.7 dynamic-slice_bitcast_fusion
  490.9 0.7 dynamic-slice_bitcast_fusion.1
  491.8 7.1 broadcast_in_dim.79
  498.9 14.3 %copy.30 = f32[1024,3584]{1,0:T(8,128)} copy(f32[1024,3584]{0,1:T(8,128)} %bitcast.50) | data formatting | bytes 29360128 | tf_op jit(solution)/shard_map/reshape | solution.py:8
  513.2 8.7 %copy.31 = f32[448,8,16,128]{3,2,1,0:T(8,128)S(1)} copy(bf16[448,8,16,128]{3,1,2,0:T(8,128)(2,1)} %bitcast.43) | data formatting | bytes 44040192
  522.0 9.7 %fusion = bf16[3584,16,128]{2,1,0:T(8,128)(2,1)} fusion(f32[448,8,16,128]{3,2,1,0:T(8,128)S(1)} %copy.31, f32[3584,16]{1,0:T(8,128)S(1)} %bitcast.54), kind=kLoop, calls=%fused_computation.1 | loop fusion | flops 14680064 | bytes 44269568 | tf_op jit(solution)/shard_map/convert_element_type | solution.py:9
  531.7 27.5 %fusion.1 = f32[1280,2048]{1,0:T(8,128)} fusion(bf16[1280,3584]{1,0:T(8,128)(2,1)} %bitcast.5, bf16[448,8,16,128]{3,2,1,0:T(8,128)(2,1)} %bitcast.52), kind=kOutput, calls=%fused_computation.4 | convolution fusion | flops 18790481920 | bytes 34340864 | tf_op jit(solution)/shard_map/dot_general | solution.py:58
  559.2 90.9 %all-to-all-done.2 = bf16[32,32,3584]{2,1,0:T(8,128)(2,1)} async-done(((bf16[32,32,3584]{2,1,0:T(8,128)(2,1)}), bf16[32,32,3584]{2,1,0:T(8,128)(2,1)}, u32[]{:S(2)}, u32[]{:S(2)}) %all-to-all-start.2) | async-done | bytes 7340064 | tf_op jit(solution)/shard_map/all_to_all | solution.py:53
  650.1 21.1 %convolution_convert_fusion = bf16[1280,3584]{1,0:T(8,128)(2,1)} fusion(f32[1024,3584]{1,0:T(8,128)} %copy.30, bf16[1024,3584]{1,0:T(8,128)(2,1)} %bitcast.16, f32[1280,2048]{1,0:T(8,128)} %fusion.1), kind=kOutput, calls=%fused_computation.2 | convolution fusion | flops 9418702848 | bytes 41680896 | tf_op jit(solution)/shard_map/dot_general | solution.py:60
  671.2 4.9 all-to-all-start.3
  676.2 140.8 %all-to-all-done.3 = bf16[16,80,3584]{2,1,0:T(8,128)(2,1)} async-done(((bf16[16,80,3584]{2,1,0:T(8,128)(2,1)}), bf16[16,80,3584]{2,1,0:T(8,128)(2,1)}, u32[]{:S(2)}, u32[]{:S(2)}) %all-to-all-start.3) | async-done | bytes 9175072 | tf_op jit(solution)/shard_map/all_to_all | solution.py:61
  816.9 6.2 convolution_select_fusion
  823.2 0.6 select_reduce_fusion
  823.9 5.9 fusion.7
  (21 shorter events, 0.7 us)
Async XLA Ops:
  0.6 1.4 copy-start
  8.1 145.8 %all-to-all-start = ((bf16[16,80,3584]{2,1,0:T(8,128)(2,1)}), bf16[16,80,3584]{2,1,0:T(8,128)(2,1)}, u32[]{:S(2)}, u32[]{:S(2)}) async-start(bf16[16,80,3584]{2,1,0:T(8,128)(2,1)} %bitcast.51), calls=%async_computation | async-start | bytes 18350080 | tf_op jit(solution)/shard_map/all_to_all | solution.py:47
  153.8 329.5 %all-to-all-start.1 = ((bf16[32,112,2048]{2,1,0:T(8,128)(2,1)}), bf16[32,112,2048]{2,1,0:T(8,128)(2,1)}, u32[]{:S(2)}, u32[]{:S(2)}) async-start(bf16[32,112,2048]{2,1,0:T(8,128)(2,1)} %pad_maximum_fusion), calls=%async_computation.1 | async-start | bytes 29360128 | tf_op jit(solution)/shard_map/all_to_all | solution.py:52
  483.3 166.8 %all-to-all-start.2 = ((bf16[32,32,3584]{2,1,0:T(8,128)(2,1)}), bf16[32,32,3584]{2,1,0:T(8,128)(2,1)}, u32[]{:S(2)}, u32[]{:S(2)}) async-start(bf16[32,32,3584]{2,1,0:T(8,128)(2,1)} %pad_maximum_fusion.1), calls=%async_computation.2 | async-start | bytes 14680064 | tf_op jit(solution)/shard_map/all_to_all | solution.py:53
  671.2 4.9 copy-start.2
  671.2 145.7 %copy-start.3 = (bf16[128,3584]{1,0:T(8,128)(2,1)S(1)}, bf16[128,3584]{1,0:T(8,128)(2,1)}, u32[]{:S(2)}) copy-start(bf16[128,3584]{1,0:T(8,128)(2,1)} %param.10) | copy-start | bytes 2752516
  671.2 145.7 %all-to-all-start.3 = ((bf16[16,80,3584]{2,1,0:T(8,128)(2,1)}), bf16[16,80,3584]{2,1,0:T(8,128)(2,1)}, u32[]{:S(2)}, u32[]{:S(2)}) async-start(bf16[16,80,3584]{2,1,0:T(8,128)(2,1)} %bitcast.53), calls=%async_computation.3 | async-start | bytes 18350080 | tf_op jit(solution)/shard_map/all_to_all | solution.py:61
  816.9 12.9 %copy-start.1 = (bf16[128,3584]{1,0:T(8,128)(2,1)S(1)}, bf16[128,3584]{1,0:T(8,128)(2,1)}, u32[]{:S(2)}) copy-start(bf16[128,3584]{1,0:T(8,128)(2,1)} %param.9) | copy-start | bytes 2752516
where the time goes:
time: 836 us; the launch traced here: 830 us
  waiting for transfers between devices  676 us (81%)
  matrix products  66.9 us (8%)
  local copies, waits for them, and re-layouts  32 us (4%)
  other arithmetic  31.3 us (4%)
  starting transfers between devices  23.2 us (3%)
    all_to_all x1, waiting for transfers between devices, shards(): lax.all_to_all(send_gate, 'expert', split_axis=0, concat_axis=0, tiled=True)  316 us
    all_to_all x1, waiting for transfers between devices, shards(): lax.all_to_all(result.reshape(arrived.shape), 'expert', split_axis=0, con...  141 us
    all_to_all x1, waiting for transfers between devices, shards(): lax.all_to_all(outgoing, 'expert', split_axis=0, concat_axis=0, tiled=Tru...  128 us
    all_to_all x1, waiting for transfers between devices, shards(): lax.all_to_all(send_down, 'expert', split_axis=0, concat_axis=0, tiled=True)  90.9 us
    dot_general x1, matrix products, shards(): hidden = jnp.dot(row_block, w_gu, preferred_element_type=jnp.float32)  27.5 us
    dot_general x1, matrix products, shards(): jnp.dot(active, w_down, preferred_element_type=jnp.float32)  21.1 us
  transfers between devices with their start and end apart: 4, of which 4 were waited for; matrix products, arithmetic and copies ran while one was open for 11% of the time, Pallas kernels for 0%

commit v1 on v0

--- a/solution.py
+++ b/solution.py
@@ -1,6 +1,10 @@
+import functools
+
 import jax
 import jax.numpy as jnp
 from jax import lax
+from jax.experimental import pallas as pl
+from jax.experimental.pallas import tpu as pltpu
 from jax.sharding import PartitionSpec as P
 
 
@@ -77,6 +81,464 @@
     return (layer_out, gate_grad)
 
 
+LANES = 128
+PAIR = 2
+RING = 4
+TILE = 512
+MESH = pl.DeviceIdType.MESH
+
+
+def fits(devices, experts, stored_rows, hidden_rows, hidden_width):
+    outer = hidden_width // LANES
+    return (
+        hidden_width % LANES == 0
+        and outer % 2 == 0
+        and devices % (2 * outer) == 0
+        and experts % PAIR == 0
+        and experts <= LANES
+        and stored_rows % 16 == 0
+        and stored_rows <= LANES
+        and hidden_rows % 16 == 0
+        and LANES % hidden_rows == 0
+    )
+
+
+def layer_kernel(
+    sizes, wgu, wdn, tok, cot,
+    out, grads, gu, dn,
+    tok_v, cot_v, acc, act, gu_v, dn_v, own_v, y_in, z_in, part, part_out, part_in,
+    a2a_s, a2a_r, x_s, x_r, p_s, p_r, own_sem, load_sem, dn_sem, dn_xs, dn_xr, dn_ps, dn_pr,
+    tok_s, tok_z, tok_y, loc_sem, ry_s, ry_r, rz_s, rz_r, gr_s, gr_r,
+):
+    outer, inner, count, rows, width = sizes
+    chips, depth = inner // 2, outer // 2
+    experts = wdn.shape[0]
+    hidden = wdn.shape[1]
+    chunks = experts // PAIR
+    devices = outer * inner
+    me = lax.axis_index("expert")
+    o, i = me // inner, me % inner
+    zz, yy, xx, c = o // 2, o % 2, i // 2, i % 2
+    place = o * chips + xx
+    partner = o * inner + xx * 2 + (1 - c)
+    y_peer = (zz * 2 + (1 - yy)) * inner + i
+    right, left = me + 2 * inner, me - 2 * inner
+
+    def group_peer(r):
+        return ((o + r) % outer) * inner + i
+
+    def x_peer(k):
+        return o * inner + ((xx + k) % chips) * 2 + c
+
+    def remote(src, dst, send, recv, device):
+        return pltpu.make_async_remote_copy(
+            src_ref=src, dst_ref=dst, send_sem=send, recv_sem=recv,
+            device_id=(device,), device_id_type=MESH,
+        )
+
+    def settle(ref, sem):
+        pltpu.make_async_copy(ref, ref, sem).wait()
+
+    stage_in = pltpu.make_async_copy(wgu.at[o], own_v, own_sem)
+    stage_in.start()
+    own_rows = pl.ds(pl.multiple_of(o * count, count), count)
+    for source, target, slot in ((tok, tok_v, 0), (cot, cot_v, 1)):
+        pltpu.make_async_copy(source, target.at[own_rows], loc_sem.at[slot]).start()
+
+    barrier = pltpu.get_barrier_semaphore()
+    for r in range(1, outer):
+        pl.semaphore_signal(barrier, inc=1, device_id=(group_peer(r),), device_id_type=MESH)
+    for k in range(1, chips):
+        pl.semaphore_signal(barrier, inc=1, device_id=(x_peer(k),), device_id_type=MESH)
+    pl.semaphore_signal(barrier, inc=1, device_id=(partner,), device_id_type=MESH)
+    pl.semaphore_wait(barrier, outer + chips - 1)
+
+    def block(ref, index):
+        return ref.at[pl.ds(pl.multiple_of(index * count, count), count)]
+
+    def spread(ref, array, line, direction, source=None):
+        target = (right, left, y_peer)[direction]
+        there = block(ref, line * 2 + yy)
+        arrive = tok_y.at[array, line] if direction == 2 else tok_z.at[array, line]
+        return remote(
+            there if source is None else source, there,
+            tok_s.at[array, direction, line], arrive, target,
+        )
+
+    arrays = ((tok_v, 0, tok), (cot_v, 1, cot))
+    for ref, array, source in arrays:
+        @pl.when(zz < depth - 1)
+        def _(ref=ref, array=array, source=source):
+            spread(ref, array, zz, 0, source).start()
+
+        @pl.when(zz > 0)
+        def _(ref=ref, array=array, source=source):
+            spread(ref, array, zz, 1, source).start()
+
+        spread(ref, array, zz, 2, source).start()
+
+    for k in range(1, chips):
+        remote(wdn, dn.at[:, i], dn_xs.at[k], dn_xr.at[k], x_peer(k)).start()
+    remote(wdn, dn.at[:, i], dn_ps.at[0], dn_pr.at[0], partner).start()
+
+    stage_in.wait()
+    stage_out = pltpu.make_async_copy(own_v, gu.at[:, place, c], own_sem)
+    stage_out.start()
+
+    def exchange(q):
+        for r in range(1, outer):
+            remote(
+                wgu.at[(o + r) % outer, pl.ds(q * PAIR, PAIR)],
+                gu.at[pl.ds(q * PAIR, PAIR), place, c],
+                a2a_s, a2a_r.at[q, r], group_peer(r),
+            ).start()
+
+    def relay(ref, array, step):
+        @pl.when(zz >= step)
+        def _():
+            line = zz - step
+            settle(block(ref, line * 2 + yy), tok_z.at[array, line])
+
+            @pl.when(zz < depth - 1)
+            def _():
+                spread(ref, array, line, 0).start()
+
+            spread(ref, array, line, 2).start()
+
+        @pl.when(zz + step < depth)
+        def _():
+            line = zz + step
+            settle(block(ref, line * 2 + yy), tok_z.at[array, line])
+
+            @pl.when(zz > 0)
+            def _():
+                spread(ref, array, line, 1).start()
+
+            spread(ref, array, line, 2).start()
+
+    ahead = depth - 1
+    exchange(0)
+    acc[...] = jnp.zeros_like(acc)
+    part[...] = jnp.zeros_like(part)
+    stage_out.wait()
+    for step in range(1, depth):
+        relay(tok_v, 0, step)
+        if step < ahead:
+            exchange(step)
+
+    def lane_pick(values, lane):
+        ids = lax.broadcasted_iota(jnp.int32, values.shape, 1)
+        return jnp.sum(jnp.where(ids == lane, values, 0.0), axis=1, keepdims=True)
+
+    tiles = outer * count // TILE
+
+    def gate_up(j):
+        slot = j % 2
+        settle(gu_v.at[slot], load_sem.at[slot])
+        for e in range(PAIR):
+            def tile(m, carry, e=e):
+                at = pl.ds(pl.multiple_of(m * TILE, TILE), TILE)
+                weights = gu_v[slot, e].reshape(devices * rows, 2 * LANES)
+                h = jnp.dot(tok_v[at, :], weights, preferred_element_type=jnp.float32)
+                g, u = h[:, :LANES], h[:, LANES:]
+                a = g / (1.0 + jnp.exp(-g)) * u
+                act[j % RING, at, e * LANES:(e + 1) * LANES] = a.astype(jnp.bfloat16)
+                return carry
+
+            lax.fori_loop(0, tiles, tile, 0)
+
+    def load_down(j):
+        for k in range(inner):
+            there = (i + k) % inner
+            source = wdn.at[pl.ds(j * PAIR, PAIR)] if k == 0 else dn.at[pl.ds(j * PAIR, PAIR), there]
+            pltpu.make_async_copy(source, dn_v.at[j % 2, :, there], dn_sem.at[j % 2]).start()
+
+    def down(j, carry):
+        slot = j % 2
+        settle(dn_v.at[slot], dn_sem.at[slot])
+
+        @pl.when(j + 1 < chunks)
+        def _():
+            load_down(j + 1)
+
+        def tile(m, carry):
+            at = pl.ds(pl.multiple_of(m * TILE, TILE), TILE)
+            weights = dn_v[slot].reshape(PAIR * inner * hidden, width)
+            v = lax.dot_general(
+                cot_v[at, :width], weights, (((1,), (1,)), ((), ())),
+                preferred_element_type=jnp.float32,
+            )
+            gates = cot_v[at, width:].astype(jnp.float32)
+            ids = lax.broadcasted_iota(jnp.int32, gates.shape, 1)
+            sums = part[at, :]
+            scaled = []
+            for e in range(PAIR):
+                a = act[j % RING, at, e * LANES:(e + 1) * LANES].astype(jnp.float32)
+                total = jnp.sum(a * v[:, e * LANES:(e + 1) * LANES], axis=1, keepdims=True)
+                sums = jnp.where(ids == j * PAIR + e, total, sums)
+                scaled.append((a * lane_pick(gates, j * PAIR + e)).astype(jnp.bfloat16))
+            part[at, :] = sums
+            lhs = jnp.concatenate(scaled, axis=1)
+            acc[at, :] += jnp.dot(lhs, weights, preferred_element_type=jnp.float32)
+            return carry
+
+        lax.fori_loop(0, tiles, tile, 0)
+        return carry
+
+    def step(q, carry):
+        @pl.when(q < depth - 1)
+        def _():
+            relay(cot_v, 1, q + 1)
+
+        @pl.when(q + ahead < chunks)
+        def _():
+            exchange(q + ahead)
+
+        for r in range(outer):
+            origin = (o + outer - r) % outer
+            piece = gu.at[pl.ds(q * PAIR, PAIR), origin * chips + xx, c]
+            if r:
+                settle(piece, a2a_r.at[q, r])
+            for k in range(1, chips):
+                remote(piece, piece, x_s.at[k], x_r.at[q, k], x_peer(k)).start()
+
+        @pl.when(q == 0)
+        def _():
+            for k in range(1, chips):
+                there = ((xx + chips - k) % chips) * 2 + c
+                settle(dn.at[:, there], dn_xr.at[k])
+                remote(dn.at[:, there], dn.at[:, there], dn_ps.at[k], dn_pr.at[k], partner).start()
+
+        @pl.when(q == 1)
+        def _():
+            pltpu.make_async_copy(tok, tok_v.at[own_rows], loc_sem.at[0]).wait()
+            for line in range(depth):
+                settle(block(tok_v, line * 2 + (1 - yy)), tok_y.at[0, line])
+
+        @pl.when(q >= 1)
+        def _():
+            gate_up(q - 1)
+
+        for k in range(1, chips):
+            settle(gu.at[pl.ds(0, PAIR), pl.ds(0, outer), 0], x_r.at[q, k])
+        mine = gu.at[pl.ds(q * PAIR, PAIR), :, c]
+        remote(mine, mine, p_s, p_r.at[q], partner).start()
+
+        @pl.when(q == depth - 1)
+        def _():
+            pltpu.make_async_copy(cot, cot_v.at[own_rows], loc_sem.at[1]).wait()
+            for line in range(depth):
+                settle(block(cot_v, line * 2 + (1 - yy)), tok_y.at[1, line])
+            for k in range(chips):
+                settle(dn.at[:, 0], dn_pr.at[k])
+            load_down(0)
+
+        begin = jnp.where(q < depth - 1, 0, jnp.minimum(2 * (q - depth + 1), q - 1))
+        end = jnp.where(q < depth - 1, 0, jnp.minimum(2 * (q - depth + 1) + 2, q))
+        lax.fori_loop(begin, end, down, 0)
+
+        settle(mine, p_r.at[q])
+        pltpu.make_async_copy(
+            gu.at[pl.ds(q * PAIR, PAIR)], gu_v.at[q % 2], load_sem.at[q % 2]
+        ).start()
+        return carry
+
+    lax.fori_loop(0, chunks, step, 0)
+    gate_up(chunks - 1)
+    down(chunks - 1, 0)
+
+    for ref, array, source in arrays:
+        for line in range(depth):
+            @pl.when((zz < depth - 1) & (line <= zz))
+            def _(ref=ref, array=array, line=line):
+                spread(ref, array, line, 0).wait_send()
+
+            @pl.when((zz > 0) & (line >= zz))
+            def _(ref=ref, array=array, line=line):
+                spread(ref, array, line, 1).wait_send()
+
+            spread(ref, array, line, 2).wait_send()
+
+    turned = part[...].T[:experts]
+    for b in range(outer):
+        part_out[b] = turned[:, b * count:(b + 1) * count]
+    for r in range(1, outer):
+        remote(
+            part_out.at[(o + r) % outer], part_in.at[r], gr_s.at[r], gr_r.at[r], group_peer(r)
+        ).start()
+
+    def sum_at(line):
+        return acc[pl.ds(pl.multiple_of((line * 2 + yy) * count, count), count), :]
+
+    def y_send(line):
+        there = pl.ds(pl.multiple_of((line * 2 + (1 - yy)) * count, count), count)
+        slot = pl.ds(pl.multiple_of(line * count, count), count)
+        tok_v[slot, :] = acc[there, :].astype(jnp.bfloat16)
+        remote(tok_v.at[slot], y_in.at[line], ry_s.at[line], ry_r.at[line], y_peer).start()
+
+    def z_send(line, direction, more):
+        slot_at = depth + jnp.where(line < zz, line, line - 1)
+        slot = pl.ds(pl.multiple_of(slot_at * count, count), count)
+        settle(y_in.at[line], ry_r.at[line])
+        total = sum_at(line) + y_in[line].astype(jnp.float32)
+
+        @pl.when(more)
+        def _():
+            settle(z_in.at[direction, line], rz_r.at[direction, line])
+            tok_v[slot, :] = (total + z_in[direction, line].astype(jnp.float32)).astype(jnp.bfloat16)
+
+        @pl.when(jnp.logical_not(more))
+        def _():
+            tok_v[slot, :] = total.astype(jnp.bfloat16)
+
+        remote(
+            tok_v.at[slot], z_in.at[direction, line], rz_s.at[line], rz_r.at[direction, line],
+            (right, left)[direction],
+        ).start()
+
+    for far in range(depth - 1, 0, -1):
+        @pl.when(zz + far < depth)
+        def _(far=far):
+            y_send(zz + far)
+
+        @pl.when(zz >= far)
+        def _(far=far):
+            y_send(zz - far)
+    y_send(zz)
+    for far in range(depth - 1, 0, -1):
+        @pl.when(zz + far < depth)
+        def _(far=far):
+            z_send(zz + far, 0, zz > 0)
+
+        @pl.when(zz >= far)
+        def _(far=far):
+            z_send(zz - far, 1, zz < depth - 1)
+    settle(y_in.at[zz], ry_r.at[zz])
+    own = pl.ds(pl.multiple_of(o * count, count), count)
+    acc[own, :] += y_in[zz].astype(jnp.float32)
+
+    @pl.when(zz > 0)
+    def _():
+        settle(z_in.at[0, zz], rz_r.at[0, zz])
+        acc[own, :] += z_in[0, zz].astype(jnp.float32)
+
+    @pl.when(zz < depth - 1)
+    def _():
+        settle(z_in.at[1, zz], rz_r.at[1, zz])
+        acc[own, :] += z_in[1, zz].astype(jnp.float32)
+
+    out[...] = acc[own, :].astype(jnp.bfloat16)
+    grads[...] = part_out[o]
+    for r in range(1, outer):
+        settle(part_in.at[r], gr_r.at[r])
+        grads[...] += part_in[r]
+
+    for r in range(1, outer):
+        settle(part_in.at[r], gr_s.at[r])
+    for line in range(depth):
+        settle(y_in.at[line], ry_s.at[line])
+
+        @pl.when(line != zz)
+        def _(line=line):
+            settle(y_in.at[line], rz_s.at[line])
+    settle(wgu.at[pl.ds(0, outer - 1)], a2a_s)
+    for k in range(1, chips):
+        settle(wgu, x_s.at[k])
+        settle(wdn, dn_xs.at[k])
+    settle(gu.at[:, :, 0], p_s)
+    for k in range(chips):
+        settle(wdn, dn_ps.at[k])
+
+
+def fast(
+    tokens, cotangent, routes, gates, previous_row, gu_payload, gu_scales, down_payload, down_scales
+):
+    count, width = tokens.shape
+    experts, rows, _ = gu_payload.shape
+    hidden = down_payload.shape[1]
+    devices = lax.axis_size("expert")
+    hidden_width = gu_payload.shape[2] // 2
+    outer = hidden_width // LANES
+    inner = devices // outer
+    chips, depth = inner // 2, outer // 2
+    device_id = lax.axis_index("expert")
+
+    ids = jnp.arange(experts, dtype=jnp.int32)
+    row_of = jnp.sum(jnp.where(routes[:, :, None] == ids, previous_row, 0), axis=2)
+    hits = row_of[:, :, None] == jnp.arange(LANES, dtype=jnp.int32)
+    dense = jnp.sum(jnp.where(hits, gates.astype(jnp.float32)[:, :, None], 0.0), axis=1)
+    cot = jnp.concatenate([cotangent, dense.astype(jnp.bfloat16)], axis=1)
+
+    first = device_id * rows // LANES
+    second = jnp.minimum(first + 1, gu_scales.shape[1] - 1)
+    in_first = ((device_id * rows + jnp.arange(rows)) // LANES == first)[None, :, None]
+    low = lax.dynamic_slice_in_dim(gu_scales, first, 1, axis=1)
+    high = lax.dynamic_slice_in_dim(gu_scales, second, 1, axis=1)
+    scale = jnp.where(in_first, low, high).reshape(experts, rows, 2, outer, 1)
+    wgu = gu_payload.reshape(experts, rows, 2, outer, LANES).astype(jnp.float32) * scale
+    wgu = wgu.astype(jnp.bfloat16).transpose(3, 0, 1, 2, 4).reshape(outer, experts, rows, 2 * LANES)
+    scale = lax.dynamic_slice_in_dim(down_scales, device_id * hidden // LANES, 1, axis=1)
+    wdn = down_payload.reshape(experts, hidden, width // LANES, LANES).astype(jnp.float32)
+    wdn = (wdn * scale[..., None]).astype(jnp.bfloat16).reshape(experts, hidden, width)
+
+    chunks = experts // PAIR
+    group = outer * count
+    bf16, f32 = jnp.bfloat16, jnp.float32
+    dma = pltpu.SemaphoreType.DMA
+    anywhere = pl.BlockSpec(memory_space=pl.ANY)
+    vmem = pl.BlockSpec(memory_space=pltpu.VMEM)
+    out, grads, _, _ = pl.pallas_call(
+        functools.partial(layer_kernel, (outer, inner, count, rows, width)),
+        out_shape=[
+            jax.ShapeDtypeStruct((count, width), bf16),
+            jax.ShapeDtypeStruct((experts, count), f32),
+            jax.ShapeDtypeStruct((experts, devices // 2, 2, rows, 2 * LANES), bf16),
+            jax.ShapeDtypeStruct((experts, inner, hidden, width), bf16),
+        ],
+        in_specs=[anywhere] * 4,
+        out_specs=[vmem, vmem, anywhere, anywhere],
+        scratch_shapes=[
+            pltpu.VMEM((group, width), bf16),
+            pltpu.VMEM((group, width + LANES), bf16),
+            pltpu.VMEM((group, width), f32),
+            pltpu.VMEM((RING, group, PAIR * LANES), bf16),
+            pltpu.VMEM((2, PAIR, devices // 2, 2, rows, 2 * LANES), bf16),
+            pltpu.VMEM((2, PAIR, inner, hidden, width), bf16),
+            pltpu.VMEM((experts, rows, 2 * LANES), bf16),
+            pltpu.VMEM((depth, count, width), bf16),
+            pltpu.VMEM((2, depth, count, width), bf16),
+            pltpu.VMEM((group, LANES), f32),
+            pltpu.VMEM((outer, experts, count), f32),
+            pltpu.VMEM((outer, experts, count), f32),
+            dma(()), dma((chunks, outer)),
+            dma((chips,)), dma((chunks, chips)),
+            dma(()), dma((chunks,)),
+            dma(()), dma((2,)), dma((2,)),
+            dma((chips,)), dma((chips,)), dma((chips,)), dma((chips,)),
+            dma((2, 3, depth)), dma((2, depth)), dma((2, depth)), dma((2,)),
+            dma((depth,)), dma((depth,)), dma((depth,)), dma((2, depth)),
+            dma((outer,)), dma((outer,)),
+        ],
+        compiler_params=pltpu.CompilerParams(
+            collective_id=0, has_side_effects=True, vmem_limit_bytes=66000000
+        ),
+    )(wgu, wdn, tokens, cot)
+    grads = grads.T
+    own = row_of[:, :, None] == ids
+    gate_grad = jnp.sum(jnp.where(own, grads[:, None, :], 0.0), axis=2)
+    return (out, gate_grad)
+
+
+def choose(devices, tokens, cotangent, routes, gates, previous_row, gu_payload, *rest):
+    down_payload = rest[1]
+    if fits(
+        devices, gu_payload.shape[0], gu_payload.shape[1], down_payload.shape[1],
+        gu_payload.shape[2] // 2,
+    ):
+        return fast(tokens, cotangent, routes, gates, previous_row, gu_payload, *rest)
+    return shards(tokens, cotangent, routes, gates, previous_row, gu_payload, *rest)
+
+
 def solution(mesh):
     in_specs = (
         P("expert", None),
@@ -90,4 +552,5 @@
         P(),
     )
     out_specs = (P("expert", None), P("expert", None))
-    return jax.shard_map(shards, mesh=mesh, in_specs=in_specs, out_specs=out_specs, check_vma=False)
+    return jax.shard_map(
+        functools.partial(choose, mesh.shape["expert"]), mesh=mesh, in_specs=in_specs, out_specs=out_specs, check_vma=False)

time: 836 us -> 534 us (0.64)
  waiting for transfers between devices: 676 us -> 0 us
  Pallas kernels: 0 us -> 475 us
  matrix products: 66.9 us -> 0 us
  starting transfers between devices: 23.2 us -> 0 us
  other arithmetic: 31.3 us -> 17.4 us
    all_to_all x4 -> x0, waiting for transfers between devices: 676 us -> none  [the longest x1 316 us: shards(): lax.all_to_all(send_gate, 'expert', split_axis=0, concat_axis=0, tiled=True)]
    pallas_call x0 -> x1, Pallas kernels: none -> 475 us  [fast(): pl.pallas_call(functools.partial(layer_kernel, (outer, inner, count, rows...]
    dot_general x6 -> x0, matrix products: 66.9 us -> none  [the longest x1 27.5 us: shards(): hidden = jnp.dot(row_block, w_gu, preferred_element_type=jnp.float32)]
    all_to_all x4 -> x0, starting transfers between devices: 23.2 us -> none  [the longest x1 6.72 us: shards(): lax.all_to_all(send_gate, 'expert', split_axis=0, concat_axis=0, tiled=True)]
    concatenate x2 -> x1, other arithmetic: 19.8 us -> 2.22 us  [fast(): cot = jnp.concatenate([cotangent, dense.astype(jnp.bfloat16)], axis=1)]
    transpose x0 -> x1, local copies, waits for them, and re-layouts: none -> 8.95 us  [fast(): wgu.astype(jnp.bfloat16).transpose(3, 0, 1, 2, 4)]
  transfers between devices with their start and end apart: 4 -> 0, of which waited for: 4 -> 0; matrix products, arithmetic and copies ran while one was open for 11% -> 0% of each run, Pallas kernels for 0% -> 0%
where the time goes in v1:
time: 534 us; the launch traced here: 530 us
  Pallas kernels  475 us (89%)
  local copies, waits for them, and re-layouts  36.8 us (7%)
  other arithmetic  17.4 us (3%)
    pallas_call x1, Pallas kernels, fast(): pl.pallas_call(functools.partial(layer_kernel, (outer, inner, count, rows...  475 us
    reshape x1, local copies, waits for them, and re-layouts, fast(): wgu.astype(jnp.bfloat16).transpose(3, 0, 1, 2, 4)  12.5 us
    unnamed x13, local copies, waits for them, and re-layouts  12.4 us

profile of v1, /device:TPU:16, one launch (start us, length us, event | category | flops | bytes accessed | tf_op | source)
XLA Modules:
  0.0 530.5 jit_solution(13165339355321525359)
XLA Ops:
  0.6 0.0 copy-start
  0.6 0.0 slice-start
  0.7 0.9 select_reduce_fusion.2
  1.7 0.1 copy.35
  1.8 0.8 copy.36
  2.6 0.4 select_reduce_fusion
  2.9 0.1 mul.35
  3.1 0.1 copy.42
  3.2 1.8 constant_dynamic-slice_fusion.2
  5.0 1.1 copy.37
  6.1 0.1 copy.31
  6.2 1.1 copy.38
  7.3 0.1 copy.33
  7.3 2.2 pad_maximum_fusion.cot
  9.6 0.8 broadcast_select_fusion
  10.4 0.0 slice-start.1
  10.4 4.8 multiply_convert_fusion.1.wdn
  15.2 7.9 %copy.39 = f32[224,8,16,128]{3,2,1,0:T(8,128)} copy(bf16[224,8,16,128]{3,1,2,0:T(8,128)(2,1)S(1)} %bitcast.18) | data formatting | bytes 22020096
  23.1 7.0 %fusion = bf16[8,16,112,2,128]{4,0,3,2,1:T(8,128)(2,1)S(1)} fusion(f32[16,112,2,8,128]{4,3,2,1,0:T(8,128)} %bitcast.15, f32[16,112,2,8]{3,2,1,0:T(2,128)S(1)} %broadcast_select_fusion), kind=kLoop, calls=%fused_computation.1 | loop fusion | flops 7340032 | bytes 22134784 | tf_op jit(solution)/shard_map/transpose | solution.py:479
  30.1 9.0 %copy.34 = bf16[8,16,112,2,128]{4,3,2,1,0:T(2,128)(2,1)} copy(bf16[8,16,112,2,128]{4,0,3,2,1:T(8,128)(2,1)S(1)} %fusion) | data formatting | bytes 14680064 | tf_op jit(solution)/shard_map/transpose | solution.py:479
  39.0 12.5 %reshape.44.wgu = bf16[8,16,112,256]{3,2,1,0:T(8,128)(2,1)} reshape(bf16[8,16,112,2,128]{4,3,2,1,0:T(2,128)(2,1)} %copy.34) | data formatting | bytes 14680064 | tf_op jit(solution)/shard_map/reshape | solution.py:479
  51.5 475.5 %shard_map.104 = (bf16[128,3584]{1,0:T(8,128)(2,1)}, f32[16,128]{1,0:T(8,128)}, bf16[16,16,2,112,256]{4,3,2,1,0:T(8,128)(2,1)}, bf16[16,4,32,3584]{3,2,1,0:T(8,128)(2,1)}) custom-call(bf16[8,16,112,256]{3,2,1,0:T(8,128)(2,1)} %reshape.44.wgu, bf16[16,32,3584]{2,1,0:T(8,128)(2,1)} %multiply_convert_fusion.1.wdn, bf16[128,3584]{1,0:T(8,128)(2,1)} %tok.1, ...), custom_call_target="tpu_custom_call" | custom-call | tf_op jit(solution)/shard_map/pallas_call | solution.py:490
  527.0 1.3 select_reduce_fusion.1
  528.3 2.2 copy.44
  (8 shorter events, 0.0 us)
Async XLA Ops:
  0.6 1.0 copy-start
  0.6 14.6 %slice-start = ((s8[7340032]{0:T(1024)(128)(4,1)}), s8[3145728]{0:T(1024)(128)(4,1)S(1)}, s32[]{:S(2)}) async-start(s8[7340032]{0:T(1024)(128)(4,1)} %bitcast.16), calls=%async_computation | async-start | bytes 6291456
  10.4 4.8 slice-start.1
  39.0 491.4 %copy-start.1 = (f32[16,8,28]{2,1,0:T(8,128)S(1)}, f32[16,8,28]{2,1,0:T(8,128)}, u32[]{:S(2)}) copy-start(f32[16,8,28]{2,1,0:T(8,128)} %param.17) | copy-start | bytes 43012

commit v2 on v1

--- a/solution.py
+++ b/solution.py
@@ -83,7 +83,8 @@
 
 LANES = 128
 PAIR = 2
-RING = 4
+AHEAD = 2
+CUTS = 8
 TILE = 512
 MESH = pl.DeviceIdType.MESH
 
@@ -95,6 +96,7 @@
         and outer % 2 == 0
         and devices % (2 * outer) == 0
         and experts % PAIR == 0
+        and experts >= 8 * PAIR
         and experts <= LANES
         and stored_rows % 16 == 0
         and stored_rows <= LANES
@@ -107,8 +109,8 @@
     sizes, wgu, wdn, tok, cot,
     out, grads, gu, dn,
     tok_v, cot_v, acc, act, gu_v, dn_v, own_v, y_in, z_in, part, part_out, part_in,
-    a2a_s, a2a_r, x_s, x_r, p_s, p_r, own_sem, load_sem, dn_sem, dn_xs, dn_xr, dn_ps, dn_pr,
-    tok_s, tok_z, tok_y, loc_sem, ry_s, ry_r, rz_s, rz_r, gr_s, gr_r,
+    a2a_s, a2a_r, own_s, own_r, x_s, x_r, p_s, p_r, own_sem, load_sem, dn_sem, dn_xs, dn_xr, dn_ps, dn_pr,
+    tok_s, tok_z, tok_y, cot_s, cot_z, cot_y, loc_sem, ry_s, ry_r, rz_s, rz_r, gr_s, gr_r,
 ):
     outer, inner, count, rows, width = sizes
     chips, depth = inner // 2, outer // 2
@@ -165,17 +167,18 @@
             tok_s.at[array, direction, line], arrive, target,
         )
 
-    arrays = ((tok_v, 0, tok), (cot_v, 1, cot))
-    for ref, array, source in arrays:
+    def offer(ref, array, source):
         @pl.when(zz < depth - 1)
-        def _(ref=ref, array=array, source=source):
+        def _():
             spread(ref, array, zz, 0, source).start()
 
         @pl.when(zz > 0)
-        def _(ref=ref, array=array, source=source):
+        def _():
             spread(ref, array, zz, 1, source).start()
 
         spread(ref, array, zz, 2, source).start()
+
+    offer(tok_v, 0, tok)
 
     for k in range(1, chips):
         remote(wdn, dn.at[:, i], dn_xs.at[k], dn_xr.at[k], x_peer(k)).start()
@@ -184,9 +187,14 @@
     stage_in.wait()
     stage_out = pltpu.make_async_copy(own_v, gu.at[:, place, c], own_sem)
     stage_out.start()
+    for k in range(1, chips):
+        piece = gu.at[:, place, c]
+        remote(wgu.at[o], piece, own_s.at[k], own_r.at[k], x_peer(k)).start()
+
+    even, odd = tuple(range(2, outer, 2)), tuple(range(1, outer, 2))
 
     def exchange(q):
-        for r in range(1, outer):
+        for r in even + odd:
             remote(
                 wgu.at[(o + r) % outer, pl.ds(q * PAIR, PAIR)],
                 gu.at[pl.ds(q * PAIR, PAIR), place, c],
@@ -216,15 +224,15 @@
 
             spread(ref, array, line, 2).start()
 
-    ahead = depth - 1
-    exchange(0)
     acc[...] = jnp.zeros_like(acc)
     part[...] = jnp.zeros_like(part)
     stage_out.wait()
     for step in range(1, depth):
         relay(tok_v, 0, step)
-        if step < ahead:
-            exchange(step)
+        if step == depth - 2:
+            exchange(0)
+    for q in range(1, AHEAD):
+        exchange(q)
 
     def lane_pick(values, lane):
         ids = lax.broadcasted_iota(jnp.int32, values.shape, 1)
@@ -239,10 +247,10 @@
             def tile(m, carry, e=e):
                 at = pl.ds(pl.multiple_of(m * TILE, TILE), TILE)
                 weights = gu_v[slot, e].reshape(devices * rows, 2 * LANES)
-                h = jnp.dot(tok_v[at, :], weights, preferred_element_type=jnp.float32)
+                h = jnp.dot(tok_v[at, :width], weights, preferred_element_type=jnp.float32)
                 g, u = h[:, :LANES], h[:, LANES:]
                 a = g / (1.0 + jnp.exp(-g)) * u
-                act[j % RING, at, e * LANES:(e + 1) * LANES] = a.astype(jnp.bfloat16)
+                act[j, at, e * LANES:(e + 1) * LANES] = a.astype(jnp.bfloat16)
                 return carry
 
             lax.fori_loop(0, tiles, tile, 0)
@@ -253,101 +261,168 @@
             source = wdn.at[pl.ds(j * PAIR, PAIR)] if k == 0 else dn.at[pl.ds(j * PAIR, PAIR), there]
             pltpu.make_async_copy(source, dn_v.at[j % 2, :, there], dn_sem.at[j % 2]).start()
 
-    def down(j, carry):
-        slot = j % 2
-        settle(dn_v.at[slot], dn_sem.at[slot])
+    def down_rows(j):
+        settle(dn_v.at[j % 2], dn_sem.at[j % 2])
 
         @pl.when(j + 1 < chunks)
         def _():
             load_down(j + 1)
+
+        return dn_v[j % 2].reshape(PAIR * inner * hidden, width)
+
+    def down(j):
+        weights = down_rows(j)
 
         def tile(m, carry):
             at = pl.ds(pl.multiple_of(m * TILE, TILE), TILE)
-            weights = dn_v[slot].reshape(PAIR * inner * hidden, width)
-            v = lax.dot_general(
-                cot_v[at, :width], weights, (((1,), (1,)), ((), ())),
-                preferred_element_type=jnp.float32,
-            )
-            gates = cot_v[at, width:].astype(jnp.float32)
-            ids = lax.broadcasted_iota(jnp.int32, gates.shape, 1)
-            sums = part[at, :]
+            gates = tok_v[at, width:].astype(jnp.float32)
             scaled = []
             for e in range(PAIR):
-                a = act[j % RING, at, e * LANES:(e + 1) * LANES].astype(jnp.float32)
-                total = jnp.sum(a * v[:, e * LANES:(e + 1) * LANES], axis=1, keepdims=True)
-                sums = jnp.where(ids == j * PAIR + e, total, sums)
+                a = act[j, at, e * LANES:(e + 1) * LANES].astype(jnp.float32)
                 scaled.append((a * lane_pick(gates, j * PAIR + e)).astype(jnp.bfloat16))
-            part[at, :] = sums
             lhs = jnp.concatenate(scaled, axis=1)
             acc[at, :] += jnp.dot(lhs, weights, preferred_element_type=jnp.float32)
             return carry
 
         lax.fori_loop(0, tiles, tile, 0)
+
+    def gate_sums(j, carry):
+        weights = down_rows(j)
+
+        def tile(m, inside):
+            at = pl.ds(pl.multiple_of(m * TILE, TILE), TILE)
+            v = lax.dot_general(
+                cot_v[at, :], weights, (((1,), (1,)), ((), ())),
+                preferred_element_type=jnp.float32,
+            )
+            sums = part[at, :]
+            ids = lax.broadcasted_iota(jnp.int32, sums.shape, 1)
+            for e in range(PAIR):
+                a = act[j, at, e * LANES:(e + 1) * LANES].astype(jnp.float32)
+                total = jnp.sum(a * v[:, e * LANES:(e + 1) * LANES], axis=1, keepdims=True)
+                sums = jnp.where(ids == j * PAIR + e, total, sums)
+            part[at, :] = sums
+            return inside
+
+        lax.fori_loop(0, tiles, tile, 0)
         return carry
 
-    def step(q, carry):
-        @pl.when(q < depth - 1)
-        def _():
-            relay(cot_v, 1, q + 1)
-
-        @pl.when(q + ahead < chunks)
-        def _():
-            exchange(q + ahead)
-
-        for r in range(outer):
+    cut = count // CUTS
+
+    def cut_at(line, side, n):
+        return cot_v.at[pl.ds(pl.multiple_of((line * 2 + side) * count + n * cut, cut), cut)]
+
+    def cut_send(line, direction, n, source=None):
+        there = cut_at(line, yy, n)
+        arrive = cot_y.at[line] if direction == 2 else cot_z.at[line, n]
+        remote(
+            there if source is None else source, there, cot_s.at[direction, line], arrive,
+            (right, left, y_peer)[direction],
+        ).start()
+
+    def cut_relay(line, direction, n):
+        settle(cut_at(line, yy, n), cot_z.at[line, n])
+
+        @pl.when((zz < depth - 1) if direction == 0 else (zz > 0))
+        def _():
+            cut_send(line, direction, n)
+
+        cut_send(line, 2, n)
+
+    def cut_step(t):
+        for k in range(1, depth):
+            n = t - k
+
+            @pl.when((n >= 0) & (n < CUTS) & (zz >= k))
+            def _(n=n, k=k):
+                cut_relay(zz - k, 0, n)
+
+            @pl.when((n >= 0) & (n < CUTS) & (zz + k < depth))
+            def _(n=n, k=k):
+                cut_relay(zz + k, 1, n)
+
+        @pl.when(t < CUTS)
+        def _():
+            source = cot.at[pl.ds(pl.multiple_of(t * cut, cut), cut)]
+
+            @pl.when(zz < depth - 1)
+            def _():
+                cut_send(zz, 0, t, source)
+
+            @pl.when(zz > 0)
+            def _():
+                cut_send(zz, 1, t, source)
+
+            cut_send(zz, 2, t, source)
+
+    def pass_on(q, steps):
+        for r in steps:
             origin = (o + outer - r) % outer
             piece = gu.at[pl.ds(q * PAIR, PAIR), origin * chips + xx, c]
-            if r:
-                settle(piece, a2a_r.at[q, r])
+            settle(piece, a2a_r.at[q, r])
             for k in range(1, chips):
                 remote(piece, piece, x_s.at[k], x_r.at[q, k], x_peer(k)).start()
 
-        @pl.when(q == 0)
+    def step(t, carry):
+        @pl.when(t + AHEAD < chunks)
+        def _():
+            exchange(t + AHEAD)
+
+        @pl.when(t < chunks)
+        def _():
+            pass_on(t, even)
+
+        @pl.when(t == 1)
         def _():
             for k in range(1, chips):
                 there = ((xx + chips - k) % chips) * 2 + c
                 settle(dn.at[:, there], dn_xr.at[k])
                 remote(dn.at[:, there], dn.at[:, there], dn_ps.at[k], dn_pr.at[k], partner).start()
-
-        @pl.when(q == 1)
+                settle(gu.at[:, 0, 0], own_r.at[k])
+
+        @pl.when(t >= 1)
+        def _():
+            for k in range(1, chips):
+                settle(gu.at[pl.ds(0, PAIR), pl.ds(0, outer - 1), 0], x_r.at[t - 1, k])
+            mine = gu.at[pl.ds((t - 1) * PAIR, PAIR), :, c]
+            remote(mine, mine, p_s, p_r.at[t - 1], partner).start()
+
+        @pl.when(t == 2)
         def _():
             pltpu.make_async_copy(tok, tok_v.at[own_rows], loc_sem.at[0]).wait()
             for line in range(depth):
                 settle(block(tok_v, line * 2 + (1 - yy)), tok_y.at[0, line])
-
-        @pl.when(q >= 1)
-        def _():
-            gate_up(q - 1)
-
-        for k in range(1, chips):
-            settle(gu.at[pl.ds(0, PAIR), pl.ds(0, outer), 0], x_r.at[q, k])
-        mine = gu.at[pl.ds(q * PAIR, PAIR), :, c]
-        remote(mine, mine, p_s, p_r.at[q], partner).start()
-
-        @pl.when(q == depth - 1)
-        def _():
-            pltpu.make_async_copy(cot, cot_v.at[own_rows], loc_sem.at[1]).wait()
-            for line in range(depth):
-                settle(block(cot_v, line * 2 + (1 - yy)), tok_y.at[1, line])
             for k in range(chips):
                 settle(dn.at[:, 0], dn_pr.at[k])
             load_down(0)
 
-        begin = jnp.where(q < depth - 1, 0, jnp.minimum(2 * (q - depth + 1), q - 1))
-        end = jnp.where(q < depth - 1, 0, jnp.minimum(2 * (q - depth + 1) + 2, q))
-        lax.fori_loop(begin, end, down, 0)
-
-        settle(mine, p_r.at[q])
-        pltpu.make_async_copy(
-            gu.at[pl.ds(q * PAIR, PAIR)], gu_v.at[q % 2], load_sem.at[q % 2]
-        ).start()
+        @pl.when(t >= 2)
+        def _():
+            gate_up(t - 2)
+            down(t - 2)
+
+        @pl.when(t < chunks)
+        def _():
+            pass_on(t, odd)
+
+        @pl.when(t >= 1)
+        def _():
+            settle(gu.at[pl.ds(0, PAIR), :, c], p_r.at[t - 1])
+            pltpu.make_async_copy(
+                gu.at[pl.ds((t - 1) * PAIR, PAIR)], gu_v.at[(t - 1) % 2], load_sem.at[(t - 1) % 2]
+            ).start()
+
+        cut_step(t)
         return carry
 
-    lax.fori_loop(0, chunks, step, 0)
+    lax.fori_loop(0, chunks + 1, step, 0)
     gate_up(chunks - 1)
-    down(chunks - 1, 0)
-
-    for ref, array, source in arrays:
+    cut_step(chunks + 1)
+    down(chunks - 1)
+    cut_step(chunks + 2)
+    load_down(0)
+
+    for ref, array in ((tok_v, 0),):
         for line in range(depth):
             @pl.when((zz < depth - 1) & (line <= zz))
             def _(ref=ref, array=array, line=line):
@@ -359,6 +434,48 @@
 
             spread(ref, array, line, 2).wait_send()
 
+    def sum_at(line):
+        return acc[pl.ds(pl.multiple_of((line * 2 + yy) * count, count), count), :]
+
+    def y_send(line):
+        there = pl.ds(pl.multiple_of((line * 2 + (1 - yy)) * count, count), count)
+        slot = pl.ds(pl.multiple_of(line * count, count), count)
+        tok_v[slot, :width] = acc[there, :].astype(jnp.bfloat16)
+        remote(tok_v.at[slot, pl.ds(0, width)], y_in.at[line], ry_s.at[line], ry_r.at[line], y_peer).start()
+
+    def z_send(line, direction, more):
+        slot_at = depth + jnp.where(line < zz, line, line - 1)
+        slot = pl.ds(pl.multiple_of(slot_at * count, count), count)
+        settle(y_in.at[line], ry_r.at[line])
+        total = sum_at(line) + y_in[line].astype(jnp.float32)
+
+        @pl.when(more)
+        def _():
+            settle(z_in.at[direction, line], rz_r.at[direction, line])
+            tok_v[slot, :width] = (total + z_in[direction, line].astype(jnp.float32)).astype(jnp.bfloat16)
+
+        @pl.when(jnp.logical_not(more))
+        def _():
+            tok_v[slot, :width] = total.astype(jnp.bfloat16)
+
+        remote(
+            tok_v.at[slot, pl.ds(0, width)], z_in.at[direction, line], rz_s.at[line], rz_r.at[direction, line],
+            (right, left)[direction],
+        ).start()
+
+    for far in range(depth - 1, 0, -1):
+        @pl.when(zz + far < depth)
+        def _(far=far):
+            y_send(zz + far)
+
+        @pl.when(zz >= far)
+        def _(far=far):
+            y_send(zz - far)
+    y_send(zz)
+    pltpu.make_async_copy(cot, cot_v.at[own_rows], loc_sem.at[1]).wait()
+    for line in range(depth):
+        settle(block(cot_v, line * 2 + (1 - yy)), cot_y.at[line])
+    lax.fori_loop(0, chunks, gate_sums, 0)
     turned = part[...].T[:experts]
     for b in range(outer):
         part_out[b] = turned[:, b * count:(b + 1) * count]
@@ -367,44 +484,6 @@
             part_out.at[(o + r) % outer], part_in.at[r], gr_s.at[r], gr_r.at[r], group_peer(r)
         ).start()
 
-    def sum_at(line):
-        return acc[pl.ds(pl.multiple_of((line * 2 + yy) * count, count), count), :]
-
-    def y_send(line):
-        there = pl.ds(pl.multiple_of((line * 2 + (1 - yy)) * count, count), count)
-        slot = pl.ds(pl.multiple_of(line * count, count), count)
-        tok_v[slot, :] = acc[there, :].astype(jnp.bfloat16)
-        remote(tok_v.at[slot], y_in.at[line], ry_s.at[line], ry_r.at[line], y_peer).start()
-
-    def z_send(line, direction, more):
-        slot_at = depth + jnp.where(line < zz, line, line - 1)
-        slot = pl.ds(pl.multiple_of(slot_at * count, count), count)
-        settle(y_in.at[line], ry_r.at[line])
-        total = sum_at(line) + y_in[line].astype(jnp.float32)
-
-        @pl.when(more)
-        def _():
-            settle(z_in.at[direction, line], rz_r.at[direction, line])
-            tok_v[slot, :] = (total + z_in[direction, line].astype(jnp.float32)).astype(jnp.bfloat16)
-
-        @pl.when(jnp.logical_not(more))
-        def _():
-            tok_v[slot, :] = total.astype(jnp.bfloat16)
-
-        remote(
-            tok_v.at[slot], z_in.at[direction, line], rz_s.at[line], rz_r.at[direction, line],
-            (right, left)[direction],
-        ).start()
-
-    for far in range(depth - 1, 0, -1):
-        @pl.when(zz + far < depth)
-        def _(far=far):
-            y_send(zz + far)
-
-        @pl.when(zz >= far)
-        def _(far=far):
-            y_send(zz - far)
-    y_send(zz)
     for far in range(depth - 1, 0, -1):
         @pl.when(zz + far < depth)
         def _(far=far):
@@ -441,9 +520,19 @@
         @pl.when(line != zz)
         def _(line=line):
             settle(y_in.at[line], rz_s.at[line])
+        @pl.when((zz < depth - 1) & (line <= zz))
+        def _(line=line):
+            settle(y_in.at[line], cot_s.at[0, line])
+
+        @pl.when((zz > 0) & (line >= zz))
+        def _(line=line):
+            settle(y_in.at[line], cot_s.at[1, line])
+
+        settle(y_in.at[line], cot_s.at[2, line])
     settle(wgu.at[pl.ds(0, outer - 1)], a2a_s)
     for k in range(1, chips):
-        settle(wgu, x_s.at[k])
+        settle(wgu.at[pl.ds(0, outer - 1)], x_s.at[k])
+        settle(wgu.at[0], own_s.at[k])
         settle(wdn, dn_xs.at[k])
     settle(gu.at[:, :, 0], p_s)
     for k in range(chips):
@@ -467,7 +556,7 @@
     row_of = jnp.sum(jnp.where(routes[:, :, None] == ids, previous_row, 0), axis=2)
     hits = row_of[:, :, None] == jnp.arange(LANES, dtype=jnp.int32)
     dense = jnp.sum(jnp.where(hits, gates.astype(jnp.float32)[:, :, None], 0.0), axis=1)
-    cot = jnp.concatenate([cotangent, dense.astype(jnp.bfloat16)], axis=1)
+    tok = jnp.concatenate([tokens, dense.astype(jnp.bfloat16)], axis=1)
 
     first = device_id * rows // LANES
     second = jnp.minimum(first + 1, gu_scales.shape[1] - 1)
@@ -498,10 +587,10 @@
         in_specs=[anywhere] * 4,
         out_specs=[vmem, vmem, anywhere, anywhere],
         scratch_shapes=[
+            pltpu.VMEM((group, width + LANES), bf16),
             pltpu.VMEM((group, width), bf16),
-            pltpu.VMEM((group, width + LANES), bf16),
             pltpu.VMEM((group, width), f32),
-            pltpu.VMEM((RING, group, PAIR * LANES), bf16),
+            pltpu.VMEM((chunks, group, PAIR * LANES), bf16),
             pltpu.VMEM((2, PAIR, devices // 2, 2, rows, 2 * LANES), bf16),
             pltpu.VMEM((2, PAIR, inner, hidden, width), bf16),
             pltpu.VMEM((experts, rows, 2 * LANES), bf16),
@@ -511,18 +600,20 @@
             pltpu.VMEM((outer, experts, count), f32),
             pltpu.VMEM((outer, experts, count), f32),
             dma(()), dma((chunks, outer)),
+            dma((chips,)), dma((chips,)),
             dma((chips,)), dma((chunks, chips)),
             dma(()), dma((chunks,)),
             dma(()), dma((2,)), dma((2,)),
             dma((chips,)), dma((chips,)), dma((chips,)), dma((chips,)),
-            dma((2, 3, depth)), dma((2, depth)), dma((2, depth)), dma((2,)),
+            dma((1, 3, depth)), dma((1, depth)), dma((1, depth)),
+            dma((3, depth)), dma((depth, CUTS)), dma((depth,)), dma((2,)),
             dma((depth,)), dma((depth,)), dma((depth,)), dma((2, depth)),
             dma((outer,)), dma((outer,)),
         ],
         compiler_params=pltpu.CompilerParams(
             collective_id=0, has_side_effects=True, vmem_limit_bytes=66000000
         ),
-    )(wgu, wdn, tokens, cot)
+    )(wgu, wdn, tok, cotangent)
     grads = grads.T
     own = row_of[:, :, None] == ids
     gate_grad = jnp.sum(jnp.where(own, grads[:, None, :], 0.0), axis=2)

time: 534 us -> 425 us (0.80)
  Pallas kernels: 475 us -> 369 us
    pallas_call x1, Pallas kernels: 475 us -> 369 us  [fast(): pl.pallas_call(functools.partial(layer_kernel, (outer, inner, count, rows...]
where the time goes in v2:
time: 425 us; the launch traced here: 424 us
  Pallas kernels  369 us (87%)
  local copies, waits for them, and re-layouts  36.8 us (9%)
  other arithmetic  17.4 us (4%)
    pallas_call x1, Pallas kernels, fast(): pl.pallas_call(functools.partial(layer_kernel, (outer, inner, count, rows...  369 us
    reshape x1, local copies, waits for them, and re-layouts, fast(): wgu.astype(jnp.bfloat16).transpose(3, 0, 1, 2, 4)  12.5 us
    unnamed x13, local copies, waits for them, and re-layouts  12.4 us
    transpose x1, local copies, waits for them, and re-layouts, fast(): wgu.astype(jnp.bfloat16).transpose(3, 0, 1, 2, 4)  8.95 us

profile of v2, /device:TPU:16, one launch (start us, length us, event | category | flops | bytes accessed | tf_op | source)
XLA Modules:
  0.0 424.4 jit_solution(2840823660396742445)
XLA Ops:
  0.6 0.0 copy-start
  0.6 0.0 slice-start
  0.7 0.9 select_reduce_fusion.2
  1.7 0.1 copy.35
  1.8 0.8 copy.36
  2.6 0.4 select_reduce_fusion
  2.9 0.1 mul.35
  3.1 0.1 copy.42
  3.2 1.8 constant_dynamic-slice_fusion.2
  5.0 1.1 copy.37
  6.1 0.1 copy.31
  6.2 1.1 copy.38
  7.3 0.1 copy.33
  7.3 2.2 pad_maximum_fusion.tok
  9.6 0.8 broadcast_select_fusion
  10.4 0.0 slice-start.1
  10.4 4.8 %multiply_convert_fusion.1.wdn = bf16[16,32,3584]{2,1,0:T(8,128)(2,1)} fusion(bf16[16,32,3584]{2,1,0:T(8,128)(2,1)} %param.16, f32[16,3584]{1,0:T(8,128)S(1)} %bitcast.20), kind=kLoop, calls=%fused_computation.2 | loop fusion | flops 5505024 | bytes 7569408 | tf_op jit(solution)/shard_map/convert_element_type | solution.py:571
  15.2 7.9 %copy.39 = f32[224,8,16,128]{3,2,1,0:T(8,128)} copy(bf16[224,8,16,128]{3,1,2,0:T(8,128)(2,1)S(1)} %bitcast.18) | data formatting | bytes 22020096
  23.1 7.0 %fusion = bf16[8,16,112,2,128]{4,0,3,2,1:T(8,128)(2,1)S(1)} fusion(f32[16,112,2,8,128]{4,3,2,1,0:T(8,128)} %bitcast.15, f32[16,112,2,8]{3,2,1,0:T(2,128)S(1)} %broadcast_select_fusion), kind=kLoop, calls=%fused_computation.1 | loop fusion | flops 7340032 | bytes 22134784 | tf_op jit(solution)/shard_map/transpose | solution.py:568
  30.1 9.0 %copy.34 = bf16[8,16,112,2,128]{4,3,2,1,0:T(2,128)(2,1)} copy(bf16[8,16,112,2,128]{4,0,3,2,1:T(8,128)(2,1)S(1)} %fusion) | data formatting | bytes 14680064 | tf_op jit(solution)/shard_map/transpose | solution.py:568
  39.0 12.5 %reshape.44.wgu = bf16[8,16,112,256]{3,2,1,0:T(8,128)(2,1)} reshape(bf16[8,16,112,2,128]{4,3,2,1,0:T(2,128)(2,1)} %copy.34) | data formatting | bytes 14680064 | tf_op jit(solution)/shard_map/reshape | solution.py:568
  51.5 369.4 %shard_map.104 = (bf16[128,3584]{1,0:T(8,128)(2,1)}, f32[16,128]{1,0:T(8,128)}, bf16[16,16,2,112,256]{4,3,2,1,0:T(8,128)(2,1)}, bf16[16,4,32,3584]{3,2,1,0:T(8,128)(2,1)}) custom-call(bf16[8,16,112,256]{3,2,1,0:T(8,128)(2,1)} %reshape.44.wgu, bf16[16,32,3584]{2,1,0:T(8,128)(2,1)} %multiply_convert_fusion.1.wdn, bf16[128,3712]{1,0:T(8,128)(2,1)} %pad_maximum_fusion.tok, ...), custom_call_target="tpu_custom_call" | custom-call | tf_op jit(solution)/shard_map/pallas_call | solution.py:579
  420.9 1.3 select_reduce_fusion.1
  422.2 2.2 copy.44
  (8 shorter events, 0.0 us)
Async XLA Ops:
  0.6 1.0 copy-start
  0.6 14.6 %slice-start = ((s8[7340032]{0:T(1024)(128)(4,1)}), s8[3145728]{0:T(1024)(128)(4,1)S(1)}, s32[]{:S(2)}) async-start(s8[7340032]{0:T(1024)(128)(4,1)} %bitcast.16), calls=%async_computation | async-start | bytes 6291456
  10.4 4.8 %slice-start.1 = ((s8[7340032]{0:T(1024)(128)(4,1)}), s8[4194304]{0:T(1024)(128)(4,1)S(1)}, s32[]{:S(2)}) async-start(s8[7340032]{0:T(1024)(128)(4,1)} %bitcast.16), calls=%async_computation.1 | async-start | bytes 8388608
  39.0 385.4 %copy-start.1 = (f32[16,8,28]{2,1,0:T(8,128)S(1)}, f32[16,8,28]{2,1,0:T(8,128)}, u32[]{:S(2)}) copy-start(f32[16,8,28]{2,1,0:T(8,128)} %param.17) | copy-start | bytes 43012

commit v3 on v2

--- a/solution.py
+++ b/solution.py
@@ -97,6 +97,7 @@
         and devices % (2 * outer) == 0
         and experts % PAIR == 0
         and experts >= 8 * PAIR
+        and experts == 2 * PAIR * (devices // outer)
         and experts <= LANES
         and stored_rows % 16 == 0
         and stored_rows <= LANES
@@ -106,17 +107,16 @@
 
 
 def layer_kernel(
-    sizes, wgu, wdn, tok, cot,
-    out, grads, gu, dn,
-    tok_v, cot_v, acc, act, gu_v, dn_v, own_v, y_in, z_in, part, part_out, part_in,
-    a2a_s, a2a_r, own_s, own_r, x_s, x_r, p_s, p_r, own_sem, load_sem, dn_sem, dn_xs, dn_xr, dn_ps, dn_pr,
+    sizes, gu_raw, dn_raw, gu_scale, dn_scale, tok, dense, cot,
+    out, grads, gu, dn, wgu,
+    tok_v, cot_v, acc, act, gu_v, dn_v, raw_v, stage, y_in, z_in, part, part_out, part_in,
+    a2a_s, a2a_r, own_s, own_r, x_s, x_r, p_s, p_r, raw_sem, put_sem, keep_sem, load_sem, dn_sem, dn_xs, dn_xr, dn_ps, dn_pr,
     tok_s, tok_z, tok_y, cot_s, cot_z, cot_y, loc_sem, ry_s, ry_r, rz_s, rz_r, gr_s, gr_r,
 ):
     outer, inner, count, rows, width = sizes
     chips, depth = inner // 2, outer // 2
-    experts = wdn.shape[0]
-    hidden = wdn.shape[1]
-    chunks = experts // PAIR
+    experts = dn_raw.shape[0]
+    hidden = dn_raw.shape[1]
     devices = outer * inner
     me = lax.axis_index("expert")
     o, i = me // inner, me % inner
@@ -141,11 +141,26 @@
     def settle(ref, sem):
         pltpu.make_async_copy(ref, ref, sem).wait()
 
-    stage_in = pltpu.make_async_copy(wgu.at[o], own_v, own_sem)
-    stage_in.start()
+    def fetch(q):
+        return pltpu.make_async_copy(
+            gu_raw.at[pl.ds(q * PAIR, PAIR)], raw_v.at[q % 2], raw_sem.at[q % 2]
+        )
+
+    half = experts // 2
+    for e in range(experts):
+        target = dn_v.at[e // half, e % half // inner, e % inner]
+        pltpu.make_async_copy(dn_raw.at[e], target, dn_sem.at[e // half]).start()
     own_rows = pl.ds(pl.multiple_of(o * count, count), count)
-    for source, target, slot in ((tok, tok_v, 0), (cot, cot_v, 1)):
-        pltpu.make_async_copy(source, target.at[own_rows], loc_sem.at[slot]).start()
+    load_tok = pltpu.make_async_copy(tok, tok_v.at[own_rows, pl.ds(0, width)], loc_sem.at[0])
+    load_tok.start()
+    load_dense = pltpu.make_async_copy(
+        dense, tok_v.at[own_rows, pl.ds(width, LANES)], loc_sem.at[1]
+    )
+    load_dense.start()
+    load_cot = pltpu.make_async_copy(cot, cot_v.at[own_rows], loc_sem.at[2])
+    load_cot.start()
+    fetch(0).start()
+    fetch(1).start()
 
     barrier = pltpu.get_barrier_semaphore()
     for r in range(1, outer):
@@ -153,6 +168,8 @@
     for k in range(1, chips):
         pl.semaphore_signal(barrier, inc=1, device_id=(x_peer(k),), device_id_type=MESH)
     pl.semaphore_signal(barrier, inc=1, device_id=(partner,), device_id_type=MESH)
+    load_tok.wait()
+    load_dense.wait()
     pl.semaphore_wait(barrier, outer + chips - 1)
 
     def block(ref, index):
@@ -178,15 +195,69 @@
 
         spread(ref, array, zz, 2, source).start()
 
-    offer(tok_v, 0, tok)
-
+    offer(tok_v, 0, None)
+
+    dn_block = me * hidden // LANES
+    for part_of in range(2):
+        settle(dn_v.at[part_of], dn_sem.at[part_of])
+
+        def scale_down(k, carry, part_of=part_of):
+            e, at = k // inner, k % inner
+            for cb in range(width // LANES):
+                lanes = slice(cb * LANES, (cb + 1) * LANES)
+                values = dn_v[part_of, e, at, :, lanes].astype(jnp.float32)
+                values = values * dn_scale[part_of * half + k, dn_block, cb]
+                dn_v[part_of, e, at, :, lanes] = values.astype(jnp.bfloat16)
+            return carry
+
+        lax.fori_loop(0, half, scale_down, 0)
+        for k in range(half):
+            pltpu.make_async_copy(
+                dn_v.at[part_of, k // inner, k % inner], dn.at[part_of * half + k, i],
+                dn_sem.at[part_of],
+            ).start()
+    for part_of in range(2):
+        settle(dn_v.at[part_of], dn_sem.at[part_of])
+    mine = dn.at[:, i]
     for k in range(1, chips):
-        remote(wdn, dn.at[:, i], dn_xs.at[k], dn_xr.at[k], x_peer(k)).start()
-    remote(wdn, dn.at[:, i], dn_ps.at[0], dn_pr.at[0], partner).start()
-
-    stage_in.wait()
-    stage_out = pltpu.make_async_copy(own_v, gu.at[:, place, c], own_sem)
-    stage_out.start()
+        remote(mine, mine, dn_xs.at[k], dn_xr.at[k], x_peer(k)).start()
+    remote(mine, mine, dn_ps.at[0], dn_pr.at[0], partner).start()
+
+    first = me * rows // LANES
+    second = jnp.minimum(first + 1, gu_scale.shape[1] - 1)
+    upper = lax.broadcasted_iota(jnp.int32, (rows, LANES), 0) < (first + 1) * LANES - me * rows
+
+    def scale_up(q, carry):
+        slot = q % 2
+        settle(raw_v.at[slot], raw_sem.at[slot])
+
+        @pl.when(q >= 2)
+        def _():
+            settle(stage.at[slot], put_sem.at[slot])
+            settle(stage.at[slot, 0], keep_sem.at[slot])
+
+        for e in range(PAIR):
+            for cb in range(2 * outer):
+                low, high = gu_scale[q * PAIR + e, first, cb], gu_scale[q * PAIR + e, second, cb]
+                values = raw_v[slot, e, :, cb * LANES:(cb + 1) * LANES].astype(jnp.float32)
+                values = (values * jnp.where(upper, low, high)).astype(jnp.bfloat16)
+                side = cb // outer * LANES
+                stage[slot, cb % outer, e, :, side:side + LANES] = values
+
+        @pl.when(q + 2 < chunks)
+        def _():
+            fetch(q + 2).start()
+
+        these = pl.ds(q * PAIR, PAIR)
+        pltpu.make_async_copy(stage.at[slot], wgu.at[:, these], put_sem.at[slot]).start()
+        pltpu.make_async_copy(stage.at[slot, o], gu.at[these, place, c], keep_sem.at[slot]).start()
+        return carry
+
+    chunks = experts // PAIR
+    lax.fori_loop(0, chunks, scale_up, 0)
+    for slot in range(2):
+        settle(stage.at[slot], put_sem.at[slot])
+        settle(stage.at[slot, 0], keep_sem.at[slot])
     for k in range(1, chips):
         piece = gu.at[:, place, c]
         remote(wgu.at[o], piece, own_s.at[k], own_r.at[k], x_peer(k)).start()
@@ -226,7 +297,6 @@
 
     acc[...] = jnp.zeros_like(acc)
     part[...] = jnp.zeros_like(part)
-    stage_out.wait()
     for step in range(1, depth):
         relay(tok_v, 0, step)
         if step == depth - 2:
@@ -256,10 +326,9 @@
             lax.fori_loop(0, tiles, tile, 0)
 
     def load_down(j):
-        for k in range(inner):
-            there = (i + k) % inner
-            source = wdn.at[pl.ds(j * PAIR, PAIR)] if k == 0 else dn.at[pl.ds(j * PAIR, PAIR), there]
-            pltpu.make_async_copy(source, dn_v.at[j % 2, :, there], dn_sem.at[j % 2]).start()
+        pltpu.make_async_copy(
+            dn.at[pl.ds(j * PAIR, PAIR)], dn_v.at[j % 2], dn_sem.at[j % 2]
+        ).start()
 
     def down_rows(j):
         settle(dn_v.at[j % 2], dn_sem.at[j % 2])
@@ -389,7 +458,6 @@
 
         @pl.when(t == 2)
         def _():
-            pltpu.make_async_copy(tok, tok_v.at[own_rows], loc_sem.at[0]).wait()
             for line in range(depth):
                 settle(block(tok_v, line * 2 + (1 - yy)), tok_y.at[0, line])
             for k in range(chips):
@@ -451,15 +519,15 @@
 
         @pl.when(more)
         def _():
-            settle(z_in.at[direction, line], rz_r.at[direction, line])
-            tok_v[slot, :width] = (total + z_in[direction, line].astype(jnp.float32)).astype(jnp.bfloat16)
+            settle(z_in.at[direction, line - 1 + direction], rz_r.at[direction, line])
+            tok_v[slot, :width] = (total + z_in[direction, line - 1 + direction].astype(jnp.float32)).astype(jnp.bfloat16)
 
         @pl.when(jnp.logical_not(more))
         def _():
             tok_v[slot, :width] = total.astype(jnp.bfloat16)
 
         remote(
-            tok_v.at[slot, pl.ds(0, width)], z_in.at[direction, line], rz_s.at[line], rz_r.at[direction, line],
+            tok_v.at[slot, pl.ds(0, width)], z_in.at[direction, line - 1 + direction], rz_s.at[line], rz_r.at[direction, line],
             (right, left)[direction],
         ).start()
 
@@ -472,7 +540,7 @@
         def _(far=far):
             y_send(zz - far)
     y_send(zz)
-    pltpu.make_async_copy(cot, cot_v.at[own_rows], loc_sem.at[1]).wait()
+    load_cot.wait()
     for line in range(depth):
         settle(block(cot_v, line * 2 + (1 - yy)), cot_y.at[line])
     lax.fori_loop(0, chunks, gate_sums, 0)
@@ -498,8 +566,8 @@
 
     @pl.when(zz > 0)
     def _():
-        settle(z_in.at[0, zz], rz_r.at[0, zz])
-        acc[own, :] += z_in[0, zz].astype(jnp.float32)
+        settle(z_in.at[0, zz - 1], rz_r.at[0, zz])
+        acc[own, :] += z_in[0, zz - 1].astype(jnp.float32)
 
     @pl.when(zz < depth - 1)
     def _():
@@ -533,10 +601,10 @@
     for k in range(1, chips):
         settle(wgu.at[pl.ds(0, outer - 1)], x_s.at[k])
         settle(wgu.at[0], own_s.at[k])
-        settle(wdn, dn_xs.at[k])
+        settle(dn.at[:, 0], dn_xs.at[k])
     settle(gu.at[:, :, 0], p_s)
     for k in range(chips):
-        settle(wdn, dn_ps.at[k])
+        settle(dn.at[:, 0], dn_ps.at[k])
 
 
 def fast(
@@ -550,42 +618,29 @@
     outer = hidden_width // LANES
     inner = devices // outer
     chips, depth = inner // 2, outer // 2
-    device_id = lax.axis_index("expert")
 
     ids = jnp.arange(experts, dtype=jnp.int32)
     row_of = jnp.sum(jnp.where(routes[:, :, None] == ids, previous_row, 0), axis=2)
     hits = row_of[:, :, None] == jnp.arange(LANES, dtype=jnp.int32)
     dense = jnp.sum(jnp.where(hits, gates.astype(jnp.float32)[:, :, None], 0.0), axis=1)
-    tok = jnp.concatenate([tokens, dense.astype(jnp.bfloat16)], axis=1)
-
-    first = device_id * rows // LANES
-    second = jnp.minimum(first + 1, gu_scales.shape[1] - 1)
-    in_first = ((device_id * rows + jnp.arange(rows)) // LANES == first)[None, :, None]
-    low = lax.dynamic_slice_in_dim(gu_scales, first, 1, axis=1)
-    high = lax.dynamic_slice_in_dim(gu_scales, second, 1, axis=1)
-    scale = jnp.where(in_first, low, high).reshape(experts, rows, 2, outer, 1)
-    wgu = gu_payload.reshape(experts, rows, 2, outer, LANES).astype(jnp.float32) * scale
-    wgu = wgu.astype(jnp.bfloat16).transpose(3, 0, 1, 2, 4).reshape(outer, experts, rows, 2 * LANES)
-    scale = lax.dynamic_slice_in_dim(down_scales, device_id * hidden // LANES, 1, axis=1)
-    wdn = down_payload.reshape(experts, hidden, width // LANES, LANES).astype(jnp.float32)
-    wdn = (wdn * scale[..., None]).astype(jnp.bfloat16).reshape(experts, hidden, width)
-
     chunks = experts // PAIR
     group = outer * count
     bf16, f32 = jnp.bfloat16, jnp.float32
     dma = pltpu.SemaphoreType.DMA
     anywhere = pl.BlockSpec(memory_space=pl.ANY)
     vmem = pl.BlockSpec(memory_space=pltpu.VMEM)
-    out, grads, _, _ = pl.pallas_call(
+    smem = pl.BlockSpec(memory_space=pltpu.SMEM)
+    out, grads, _, _, _ = pl.pallas_call(
         functools.partial(layer_kernel, (outer, inner, count, rows, width)),
         out_shape=[
             jax.ShapeDtypeStruct((count, width), bf16),
             jax.ShapeDtypeStruct((experts, count), f32),
             jax.ShapeDtypeStruct((experts, devices // 2, 2, rows, 2 * LANES), bf16),
             jax.ShapeDtypeStruct((experts, inner, hidden, width), bf16),
+            jax.ShapeDtypeStruct((outer, experts, rows, 2 * LANES), bf16),
         ],
-        in_specs=[anywhere] * 4,
-        out_specs=[vmem, vmem, anywhere, anywhere],
+        in_specs=[anywhere, anywhere, smem, smem, anywhere, anywhere, anywhere],
+        out_specs=[vmem, vmem, anywhere, anywhere, anywhere],
         scratch_shapes=[
             pltpu.VMEM((group, width + LANES), bf16),
             pltpu.VMEM((group, width), bf16),
@@ -593,9 +648,10 @@
             pltpu.VMEM((chunks, group, PAIR * LANES), bf16),
             pltpu.VMEM((2, PAIR, devices // 2, 2, rows, 2 * LANES), bf16),
             pltpu.VMEM((2, PAIR, inner, hidden, width), bf16),
-            pltpu.VMEM((experts, rows, 2 * LANES), bf16),
+            pltpu.VMEM((2, PAIR, rows, 2 * hidden_width), bf16),
+            pltpu.VMEM((2, outer, PAIR, rows, 2 * LANES), bf16),
             pltpu.VMEM((depth, count, width), bf16),
-            pltpu.VMEM((2, depth, count, width), bf16),
+            pltpu.VMEM((2, depth - 1, count, width), bf16),
             pltpu.VMEM((group, LANES), f32),
             pltpu.VMEM((outer, experts, count), f32),
             pltpu.VMEM((outer, experts, count), f32),
@@ -603,17 +659,19 @@
             dma((chips,)), dma((chips,)),
             dma((chips,)), dma((chunks, chips)),
             dma(()), dma((chunks,)),
-            dma(()), dma((2,)), dma((2,)),
+            dma((2,)), dma((2,)), dma((2,)), dma((2,)), dma((2,)),
             dma((chips,)), dma((chips,)), dma((chips,)), dma((chips,)),
             dma((1, 3, depth)), dma((1, depth)), dma((1, depth)),
-            dma((3, depth)), dma((depth, CUTS)), dma((depth,)), dma((2,)),
+            dma((3, depth)), dma((depth, CUTS)), dma((depth,)), dma((3,)),
             dma((depth,)), dma((depth,)), dma((depth,)), dma((2, depth)),
             dma((outer,)), dma((outer,)),
         ],
         compiler_params=pltpu.CompilerParams(
-            collective_id=0, has_side_effects=True, vmem_limit_bytes=66000000
+            collective_id=0, has_side_effects=True, vmem_limit_bytes=67000000
         ),
-    )(wgu, wdn, tok, cotangent)
+    )(
+        gu_payload, down_payload, gu_scales, down_scales, tokens, dense.astype(bf16), cotangent
+    )
     grads = grads.T
     own = row_of[:, :, None] == ids
     gate_grad = jnp.sum(jnp.where(own, grads[:, None, :], 0.0), axis=2)

time: 425 us -> 384 us (0.904)
  local copies, waits for them, and re-layouts: 36.8 us -> 4.82 us
  other arithmetic: 17.4 us -> 3.06 us
  Pallas kernels: 369 us -> 375 us
    reshape x1 -> x0, local copies, waits for them, and re-layouts: 12.5 us -> none  [fast(): wgu.astype(jnp.bfloat16).transpose(3, 0, 1, 2, 4)]
    transpose x1 -> x0, local copies, waits for them, and re-layouts: 8.95 us -> none  [fast(): wgu.astype(jnp.bfloat16).transpose(3, 0, 1, 2, 4)]
    unnamed x13 -> x2, local copies, waits for them, and re-layouts: 12.4 us -> 3.94 us
    transpose x1 -> x0, other arithmetic: 6.97 us -> none  [fast(): wgu.astype(jnp.bfloat16).transpose(3, 0, 1, 2, 4)]
    pallas_call x1, Pallas kernels: 369 us -> 375 us  [fast(): pl.pallas_call(functools.partial(layer_kernel, (outer, inner, count, rows...]
    convert_element_type x1 -> x0, other arithmetic: 4.81 us -> none  [fast(): (wdn * scale[..., None]).astype(jnp.bfloat16)]
where the time goes in v3:
time: 384 us
  Pallas kernels  375 us (98%)
  local copies, waits for them, and re-layouts  4.82 us (1%)
    pallas_call x1, Pallas kernels, fast(): pl.pallas_call(functools.partial(layer_kernel, (outer, inner, count, rows...  375 us

profile of v3, /device:TPU:16, one launch (start us, length us, event | category | flops | bytes accessed | tf_op | source)
XLA Modules:
  0.0 383.9 jit_solution(8367684857719330078)
XLA Ops:
  0.6 0.8 select_reduce_fusion.2
  1.4 0.1 copy.15
  1.5 0.8 copy.16
  2.3 1.0 select_reduce_fusion.dense
  3.3 1.8 copy.17.gu_scale
  5.1 375.3 %shard_map.104 = (bf16[128,3584]{1,0:T(8,128)(2,1)}, f32[16,128]{1,0:T(8,128)}, bf16[16,16,2,112,256]{4,3,2,1,0:T(8,128)(2,1)}, bf16[16,4,32,3584]{3,2,1,0:T(8,128)(2,1)}, bf16[8,16,112,256]{3,2,1,0:T(8,128)(2,1)}) custom-call(bf16[16,112,2048]{2,1,0:T(8,128)(2,1)} %gu_raw.1, bf16[16,32,3584]{2,1,0:T(8,128)(2,1)} %dn_raw.1, f32[16,28,16]{2,1,0:T(8,128)} %copy.17.gu_scale, ...), custom_call_target="tpu_custom_call" | custom-call | tf_op jit(solution)/shard_map/pallas_call | solution.py:633
  380.4 1.3 select_reduce_fusion.1
  381.7 2.2 copy.19

commit v4 on v3

--- a/solution.py
+++ b/solution.py
@@ -107,9 +107,9 @@
 
 
 def layer_kernel(
-    sizes, gu_raw, dn_raw, gu_scale, dn_scale, tok, dense, cot,
+    sizes, gu_raw, dn_raw, gu_steps, dn_steps, tok, dense, cot,
     out, grads, gu, dn, wgu,
-    tok_v, cot_v, acc, act, gu_v, dn_v, raw_v, stage, y_in, z_in, part, part_out, part_in,
+    gu_scale, dn_scale, tok_v, cot_v, acc, act, gu_v, dn_v, raw_v, stage, y_in, z_in, part, part_out, part_in,
     a2a_s, a2a_r, own_s, own_r, x_s, x_r, p_s, p_r, raw_sem, put_sem, keep_sem, load_sem, dn_sem, dn_xs, dn_xr, dn_ps, dn_pr,
     tok_s, tok_z, tok_y, cot_s, cot_z, cot_y, loc_sem, ry_s, ry_r, rz_s, rz_r, gr_s, gr_r,
 ):
@@ -159,6 +159,12 @@
     load_dense.start()
     load_cot = pltpu.make_async_copy(cot, cot_v.at[own_rows], loc_sem.at[2])
     load_cot.start()
+    load_scales = (
+        pltpu.make_async_copy(dn_steps, dn_scale, loc_sem.at[3]),
+        pltpu.make_async_copy(gu_steps, gu_scale, loc_sem.at[4]),
+    )
+    for load in load_scales:
+        load.start()
     fetch(0).start()
     fetch(1).start()
 
@@ -170,6 +176,8 @@
     pl.semaphore_signal(barrier, inc=1, device_id=(partner,), device_id_type=MESH)
     load_tok.wait()
     load_dense.wait()
+    for load in load_scales:
+        load.wait()
     pl.semaphore_wait(barrier, outer + chips - 1)
 
     def block(ref, index):
@@ -197,6 +205,12 @@
 
     offer(tok_v, 0, None)
 
+    def share_down(part_of):
+        mine = dn.at[pl.ds(part_of * half, half), i]
+        for k in range(1, chips):
+            remote(mine, mine, dn_xs.at[k], dn_xr.at[k], x_peer(k)).start()
+        remote(mine, mine, dn_ps.at[0], dn_pr.at[0], partner).start()
+
     dn_block = me * hidden // LANES
     for part_of in range(2):
         settle(dn_v.at[part_of], dn_sem.at[part_of])
@@ -216,12 +230,11 @@
                 dn_v.at[part_of, k // inner, k % inner], dn.at[part_of * half + k, i],
                 dn_sem.at[part_of],
             ).start()
-    for part_of in range(2):
-        settle(dn_v.at[part_of], dn_sem.at[part_of])
-    mine = dn.at[:, i]
-    for k in range(1, chips):
-        remote(mine, mine, dn_xs.at[k], dn_xr.at[k], x_peer(k)).start()
-    remote(mine, mine, dn_ps.at[0], dn_pr.at[0], partner).start()
+        if part_of:
+            settle(dn_v.at[0], dn_sem.at[0])
+            share_down(0)
+    settle(dn_v.at[1], dn_sem.at[1])
+    share_down(1)
 
     first = me * rows // LANES
     second = jnp.minimum(first + 1, gu_scale.shape[1] - 1)
@@ -433,13 +446,13 @@
                 remote(piece, piece, x_s.at[k], x_r.at[q, k], x_peer(k)).start()
 
     def step(t, carry):
+        @pl.when(t < chunks)
+        def _():
+            pass_on(t, even)
+
         @pl.when(t + AHEAD < chunks)
         def _():
             exchange(t + AHEAD)
-
-        @pl.when(t < chunks)
-        def _():
-            pass_on(t, even)
 
         @pl.when(t == 1)
         def _():
@@ -629,7 +642,6 @@
     dma = pltpu.SemaphoreType.DMA
     anywhere = pl.BlockSpec(memory_space=pl.ANY)
     vmem = pl.BlockSpec(memory_space=pltpu.VMEM)
-    smem = pl.BlockSpec(memory_space=pltpu.SMEM)
     out, grads, _, _, _ = pl.pallas_call(
         functools.partial(layer_kernel, (outer, inner, count, rows, width)),
         out_shape=[
@@ -639,9 +651,11 @@
             jax.ShapeDtypeStruct((experts, inner, hidden, width), bf16),
             jax.ShapeDtypeStruct((outer, experts, rows, 2 * LANES), bf16),
         ],
-        in_specs=[anywhere, anywhere, smem, smem, anywhere, anywhere, anywhere],
+        in_specs=[anywhere, anywhere, anywhere, anywhere, anywhere, anywhere, anywhere],
         out_specs=[vmem, vmem, anywhere, anywhere, anywhere],
         scratch_shapes=[
+            pltpu.SMEM(gu_scales.shape, f32),
+            pltpu.SMEM(down_scales.shape, f32),
             pltpu.VMEM((group, width + LANES), bf16),
             pltpu.VMEM((group, width), bf16),
             pltpu.VMEM((group, width), f32),
@@ -662,7 +676,7 @@
             dma((2,)), dma((2,)), dma((2,)), dma((2,)), dma((2,)),
             dma((chips,)), dma((chips,)), dma((chips,)), dma((chips,)),
             dma((1, 3, depth)), dma((1, depth)), dma((1, depth)),
-            dma((3, depth)), dma((depth, CUTS)), dma((depth,)), dma((3,)),
+            dma((3, depth)), dma((depth, CUTS)), dma((depth,)), dma((5,)),
             dma((depth,)), dma((depth,)), dma((depth,)), dma((2, depth)),
             dma((outer,)), dma((outer,)),
         ],

time: 384 us -> 380 us (0.990)
  Pallas kernels: 375 us -> 371 us
    pallas_call x1, Pallas kernels: 375 us -> 371 us  [fast(): pl.pallas_call(functools.partial(layer_kernel, (outer, inner, count, rows...]
where the time goes in v4:
time: 380 us; the launch traced here: 379 us
  Pallas kernels  371 us (98%)
  local copies, waits for them, and re-layouts  4.82 us (1%)
    pallas_call x1, Pallas kernels, fast(): pl.pallas_call(functools.partial(layer_kernel, (outer, inner, count, rows...  371 us

profile of v4, /device:TPU:16, one launch (start us, length us, event | category | flops | bytes accessed | tf_op | source)
XLA Modules:
  0.0 379.2 jit_solution(6120187015968493443)
XLA Ops:
  0.6 0.8 select_reduce_fusion.2
  1.4 0.1 copy.15
  1.5 0.8 copy.16
  2.3 1.0 select_reduce_fusion.dense
  3.3 1.8 copy.17.gu_steps
  5.1 370.7 %shard_map.104 = (bf16[128,3584]{1,0:T(8,128)(2,1)}, f32[16,128]{1,0:T(8,128)}, bf16[16,16,2,112,256]{4,3,2,1,0:T(8,128)(2,1)}, bf16[16,4,32,3584]{3,2,1,0:T(8,128)(2,1)}, bf16[8,16,112,256]{3,2,1,0:T(8,128)(2,1)}) custom-call(bf16[16,112,2048]{2,1,0:T(8,128)(2,1)} %gu_raw.1, bf16[16,32,3584]{2,1,0:T(8,128)(2,1)} %dn_raw.1, f32[16,28,16]{2,1,0:T(8,128)} %copy.17.gu_steps, ...), custom_call_target="tpu_custom_call" | custom-call | tf_op jit(solution)/shard_map/pallas_call | solution.py:645
  375.8 1.3 select_reduce_fusion.1
  377.1 2.2 copy.19
